TPU v7x, 32 devices: a whole 2x2x4 slice. The times are simulated.
32 devices in a mesh: img: 2 (over x), sp: 2 (over core), tp: 8 (over z, y).
Axes of the slice: x: 2, y: 2, z: 4, core: 2. Of those that a mesh axis runs over, the one named last changes fastest.
Arguments:
- tokens: bfloat16 [16, 32, 6144], P(('img', 'tp'), 'sp'), parts along dimension 0, may hold values from -6 to 6
- up_weight: bfloat16 [6144, 24576], P('sp', 'tp'), may hold values from -0.078125 to 0.078125
- up_bias: float32 [24576], P('tp'), may hold values from -3 to 3
- conv_weight: float32 [3, 3, 24576], P(None, None, 'tp'), may hold values from -2 to 2
- conv_bias: float32 [24576], P('tp'), may hold values from -3 to 3
- down_weight: bfloat16 [24576, 6144], P('tp', 'sp'), may hold values from -0.0390625 to 0.0390625
- down_bias: float32 [6144], replicated, may hold values from -3 to 3
Outputs:
- projected: bfloat16 [16, 32, 6144], P(('img', 'tp'), 'sp'), parts along dimension 0
There are 2 independent parts, one for each index of `img`. A program takes and returns all parts, laid end to end along the dimension named above; an argument that names none is the same for every part. Nothing has to cross between parts.
All inputs are finite; a program needn't handle non-finite values.
Results may differ from a plain program's by a relative error of at most 0.0053.
Values may be sent and summed in bfloat16 or wider, within the bound.
No kernel may reach another device: no remote copies, remote signals or barrier semaphores. Data moves between devices by JAX's collectives and lax.ppermute only.
A program may use at most 256 MiB of HBM per device.

v0:
```python
import jax
import jax.numpy as jnp
from jax import lax
from jax.sharding import PartitionSpec as P


def extended(block, sides, width):
    for axis, dim in sides:
        count = lax.axis_size(axis)
        forward = [(i, i + 1) for i in range(count - 1)]
        backward = [(target, source) for source, target in forward]
        low = lax.ppermute(
            lax.slice_in_dim(block, block.shape[dim] - width, None, axis=dim), axis, forward
        )
        high = lax.ppermute(lax.slice_in_dim(block, 0, width, axis=dim), axis, backward)
        block = jnp.concatenate([low, block, high], axis=dim)
    return block


def depthwise(hidden, conv_weight, conv_bias):
    padded = extended(hidden, (("sp", 1),), 1)
    padded = jnp.pad(padded, ((1, 1), (0, 0), (0, 0)))
    extent_x = hidden.shape[0]
    extent_y = hidden.shape[1]
    summed = jnp.zeros(hidden.shape, jnp.float32) + conv_bias
    for offset_x in range(3):
        for offset_y in range(3):
            window = padded[offset_x : offset_x + extent_x, offset_y : offset_y + extent_y]
            summed = summed + window.astype(jnp.float32) * conv_weight[offset_x, offset_y]
    return jax.nn.gelu(summed, approximate=False).astype(jnp.bfloat16)


def local(tokens, up_weight, up_bias, conv_weight, conv_bias, down_weight, down_bias):
    col_count = tokens.shape[0]
    row_count = tokens.shape[1]
    width_model = tokens.shape[2]
    hidden_dev = up_weight.shape[1]
    up_full, down_full = (
        lax.all_gather(up_weight, "sp", axis=0, tiled=True),
        lax.all_gather(down_weight, "sp", axis=1, tiled=True),
    )
    piece = lax.all_gather(tokens, "tp", axis=0, tiled=True)
    flat_piece = piece.reshape(-1, width_model)
    lifted = jnp.dot(flat_piece, up_full, preferred_element_type=jnp.float32) + up_bias
    hidden = lifted.astype(jnp.bfloat16).reshape(piece.shape[0], row_count, hidden_dev)
    mixed = depthwise(hidden, conv_weight, conv_bias)
    product = jnp.dot(mixed.reshape(-1, hidden_dev), down_full, preferred_element_type=jnp.float32)
    summed_terms = lax.psum_scatter(
        product.reshape(col_count * lax.axis_size("tp"), row_count, width_model),
        "tp",
        scatter_dimension=0,
        tiled=True,
    )
    return (summed_terms + down_bias).astype(jnp.bfloat16)


def solution(mesh):
    placed = (
        P(("img", "tp"), "sp", None),
        P("sp", "tp"),
        P("tp"),
        P(None, None, "tp"),
        P("tp"),
        P("tp", "sp"),
        P(),
    )
    return jax.shard_map(
        local, mesh=mesh, in_specs=placed, out_specs=P(("img", "tp"), "sp", None), check_vma=False
    )
```

profile of v0, /device:TPU:0, one launch (start us, length us, event | category | flops | bytes accessed | tf_op | source)
XLA Modules:
  0.0 277.0 jit_solution(13013426997348441983)
XLA Ops:
  6.5 0.0 all-gather.4.cloned.1.call-start
  6.5 0.7 all-gather.4.cloned.1.call-update
  7.3 0.0 all-gather.6.cloned.1.call-start
  7.3 0.7 all-gather.6.cloned.1.call-update
  8.0 0.0 copy-start.2
  8.0 0.0 all-gather.8.cloned.1.call-start
  8.1 0.7 all-gather.8.cloned.1.call-update
  8.8 0.0 reduce-scatter.2.cloned.1.call-start
  8.8 47.7 %all-gather.4.cloned.1.call-done = bf16[8,16,6144]{2,1,0:T(8,128)(2,1)} async-done(((bf16[1,16,6144]{2,1,0:T(8,128)(2,1)}), bf16[8,16,6144]{2,1,0:T(8,128)(2,1)}) %all-gather.4.cloned.1.call-update) | async-done | bytes 1572880 | tf_op jit(solution)/shard_map/all_gather | solution.py:42
  56.5 58.2 %all-gather.6.cloned.1.call-done = bf16[6144,3072]{1,0:T(8,128)(2,1)} async-done(((bf16[3072,3072]{1,0:T(8,128)(2,1)}), bf16[6144,3072]{1,0:T(8,128)(2,1)}) %all-gather.6.cloned.1.call-update) | async-done | bytes 37748752 | tf_op jit(solution)/shard_map/all_gather | solution.py:39
  114.7 0.0 copy-done.2
  114.7 0.0 copy-start
  114.7 18.7 %fusion.2 = bf16[128,3072]{1,0:T(8,128)(2,1)S(1)} fusion(bf16[128,6144]{1,0:T(8,128)(2,1)} %bitcast.19, bf16[6144,3072]{1,0:T(8,128)(2,1)} %all-gather.6.cloned.1.call-done, f32[3072]{0:T(1024)S(1)} %copy-done.2), kind=kOutput, calls=%fused_computation.5 | convolution fusion | flops 4832624640 | bytes 40120320 | tf_op jit(solution)/shard_map/dot_general | solution.py:44
  133.3 0.0 copy-start.3
  133.3 0.2 fusion.99
  133.5 2.0 collective-permute-start
  135.5 1.3 collective-permute-start.1
  136.8 0.0 copy-done
  136.8 0.1 fusion.100
  136.9 0.0 collective-permute-done
  136.9 1.8 collective-permute-done.1
  138.7 0.5 fusion.18
  139.2 36.0 %all-gather.8.cloned.1.call-done = bf16[3072,6144]{1,0:T(8,128)(2,1)} async-done(((bf16[3072,3072]{1,0:T(8,128)(2,1)}), bf16[3072,6144]{1,0:T(8,128)(2,1)}) %all-gather.8.cloned.1.call-update) | async-done | bytes 37748752 | tf_op jit(solution)/shard_map/all_gather | solution.py:40
  175.2 0.0 copy-done.3
  175.2 18.0 %fusion = f32[8,16,6144]{2,1,0:T(8,128)} fusion(bf16[3072,6144]{1,0:T(8,128)(2,1)} %all-gather.8.cloned.1.call-done, bf16[8,16,3072]{2,1,0:T(8,128)(2,1)S(1)} %bitcast.18, bf16[10,18,3072]{2,1,0:T(8,128)(2,1)S(1)} %fusion.18, bf16[8,1,3072]{2,1,0:T(2,128)(2,1)S(1)} %collective-permute-done.1, bf16[8,1,3072]{2,1,0:T(2,128)(2,1)S(1)} %collective-permute-done, ...), kind=kOutput, calls=%fused_computation | convolution fusion | flops 4870373376 | bytes 46718976 | tf_op jit(solution)/shard_map/dot_general | solution.py:47
  193.1 0.0 copy-start.1
  193.1 0.0 reduce-scatter.2.cloned.1.call-update
  193.2 75.6 %reduce-scatter.2.cloned.1.call-done = f32[1,16,6144]{2,1,0:T(8,128)} async-done(((f32[8,16,6144]{2,1,0:T(8,128)}), f32[1,16,6144]{2,1,0:T(8,128)}) %reduce-scatter.2.cloned.1.call-update) | async-done | bytes 393232 | tf_op jit(solution)/shard_map/reduce_scatter | solution.py:48
  268.7 0.0 copy-done.1
  268.7 1.7 add_convert_fusion
Async XLA Ops:
  6.5 49.9 %all-gather.4.cloned.1.call-start = ((), (), s32[]{:S(2)}) async-start(), calls=%async_computation.1 | async-start | bytes 1769472 | tf_op jit(solution)/shard_map/all_gather | solution.py:42
  7.3 107.4 %all-gather.6.cloned.1.call-start = ((), (), s32[]{:S(2)}) async-start(), calls=%async_computation.2 | async-start | bytes 56623104 | tf_op jit(solution)/shard_map/all_gather | solution.py:39
  8.0 106.7 %copy-start.2 = (f32[3072]{0:T(1024)S(1)}, f32[3072]{0:T(1024)}, u32[]{:S(2)}) copy-start(f32[3072]{0:T(1024)} %param.9) | copy-start | bytes 36868
  8.0 167.2 %all-gather.8.cloned.1.call-start = ((), (), s32[]{:S(2)}) async-start(), calls=%async_computation.3 | async-start | bytes 56623104 | tf_op jit(solution)/shard_map/all_gather | solution.py:40
  8.8 260.0 %reduce-scatter.2.cloned.1.call-start = ((), (), s32[]{:S(2)}) async-start(), calls=%async_computation.4 | async-start | bytes 3538944 | tf_op jit(solution)/shard_map/reduce_scatter | solution.py:48
  114.7 22.1 %copy-start = (f32[3,3,3072]{2,1,0:T(4,128)S(1)}, f32[3,3,3072]{2,1,0:T(4,128)}, u32[]{:S(2)}) copy-start(f32[3,3,3072]{2,1,0:T(4,128)} %param.10) | copy-start | bytes 331780
  133.3 41.8 %copy-start.3 = (f32[3072]{0:T(1024)S(1)}, f32[3072]{0:T(1024)}, u32[]{:S(2)}) copy-start(f32[3072]{0:T(1024)} %param.11) | copy-start | bytes 36868
  133.5 3.4 %collective-permute-start = (bf16[8,1,3072]{2,1,0:T(2,128)(2,1)S(1)}, bf16[8,1,3072]{2,1,0:T(2,128)(2,1)S(1)}, u32[]{:S(2)}, u32[]{:S(2)}) collective-permute-start(bf16[8,1,3072]{2,1,0:T(2,128)(2,1)S(1)} %get-tuple-element.5), channel_id=1, source_target_pairs={{0,8},{1,9},{2,10},{3,11},{4,12},{5,13},{6,14},{7,15},{16,24},{17,... | collective-permute-start | bytes 147464 | tf_op jit(solution)/shard_map/ppermute | solution.py:12
  135.5 3.2 %collective-permute-start.1 = (bf16[8,1,3072]{2,1,0:T(2,128)(2,1)S(1)}, bf16[8,1,3072]{2,1,0:T(2,128)(2,1)S(1)}, u32[]{:S(2)}, u32[]{:S(2)}) collective-permute-start(bf16[8,1,3072]{2,1,0:T(2,128)(2,1)S(1)} %get-tuple-element.6), channel_id=1, source_target_pairs={{8,0},{9,1},{10,2},{11,3},{12,4},{13,5},{14,6},{15,7},{24,16},{25,... | collective-permute-start | bytes 147464 | tf_op jit(solution)/shard_map/ppermute | solution.py:15
  193.1 75.6 %copy-start.1 = (f32[6144]{0:T(1024)S(1)}, f32[6144]{0:T(1024)}, u32[]{:S(2)}) copy-start(f32[6144]{0:T(1024)} %param.13) | copy-start | bytes 73732
Sparse Core Ops, SparseCore 0:
  9.5 46.8 all-gather.3
  58.0 56.5 all-gather.5
  116.2 58.9 all-gather.7
  193.3 75.3 reduce-scatter.1
where the time goes:
time: 277 us
  waiting for transfers between devices  221 us (80%)
  matrix products  36.6 us (13%)
  between operations  13.2 us (5%)
  starting transfers between devices  3.38 us (1%)
    reduce_scatter x1, waiting for transfers between devices, local(): lax.psum_scatter(product.reshape(col_count * lax.axis_size('tp'), row_cou...  75.6 us
    all_gather x1, waiting for transfers between devices, local(): lax.all_gather(up_weight, 'sp', axis=0, tiled=True)  58.2 us
    all_gather x1, waiting for transfers between devices, local(): piece = lax.all_gather(tokens, 'tp', axis=0, tiled=True)  47.7 us
    all_gather x1, waiting for transfers between devices, local(): lax.all_gather(down_weight, 'sp', axis=1, tiled=True)  36 us
    dot_general x1, matrix products, local(): jnp.dot(flat_piece, up_full, preferred_element_type=jnp.float32) + up_bias  18.7 us
    dot_general x1, matrix products, local(): jnp.dot(mixed.reshape(-1, hidden_dev), down_full, preferred_element_type=...  18 us
  transfers between devices with their start and end apart: 6, of which 5 were waited for; matrix products, arithmetic and copies ran while one was open for 7% of the time, Pallas kernels for 0%

commit v1 on v0

--- a/solution.py
+++ b/solution.py
@@ -2,6 +2,24 @@
 import jax.numpy as jnp
 from jax import lax
 from jax.sharding import PartitionSpec as P
+
+
+def gather_around(array, axis, dim):
+    ways, here, step = (lax.axis_size(axis), lax.axis_index(axis), array.shape[dim])
+    dims = [n * ways if d == dim else n for d, n in enumerate(array.shape)]
+    full = lax.dynamic_update_slice_in_dim(
+        jnp.zeros(dims, array.dtype), array, here * step, axis=dim
+    )
+    going_up = going_down = array
+    for far in range(1, ways // 2 + 1):
+        going_up = lax.ppermute(going_up, axis, [(d, (d + 1) % ways) for d in range(ways)])
+        full = lax.dynamic_update_slice_in_dim(full, going_up, (here - far) % ways * step, axis=dim)
+        if 2 * far < ways:
+            going_down = lax.ppermute(going_down, axis, [(d, (d - 1) % ways) for d in range(ways)])
+            full = lax.dynamic_update_slice_in_dim(
+                full, going_down, (here + far) % ways * step, axis=dim
+            )
+    return full
 
 
 def extended(block, sides, width):
@@ -39,7 +57,7 @@
         lax.all_gather(up_weight, "sp", axis=0, tiled=True),
         lax.all_gather(down_weight, "sp", axis=1, tiled=True),
     )
-    piece = lax.all_gather(tokens, "tp", axis=0, tiled=True)
+    piece = gather_around(tokens, "tp", 0)
     flat_piece = piece.reshape(-1, width_model)
     lifted = jnp.dot(flat_piece, up_full, preferred_element_type=jnp.float32) + up_bias
     hidden = lifted.astype(jnp.bfloat16).reshape(piece.shape[0], row_count, hidden_dev)

time: 277 us -> 232 us (0.84)
  waiting for transfers between devices: 221 us -> 157 us
  starting transfers between devices: 3.38 us -> 22.8 us
    all_gather x1 -> x0, waiting for transfers between devices: 47.7 us -> none  [local(): piece = lax.all_gather(tokens, 'tp', axis=0, tiled=True)]
    all_gather x1, waiting for transfers between devices: 58.2 us -> 19.2 us  [local(): lax.all_gather(up_weight, 'sp', axis=0, tiled=True)]
    ppermute x0 -> x7, waiting for transfers between devices: none -> 22.1 us  [the longest x4 20.2 us: gather_around(): lax.ppermute(going_up, axis, [(d, (d + 1) % ways) for d in range(ways)])]
    ppermute x0 -> x7, starting transfers between devices: none -> 19.5 us  [the longest x3 10.5 us: gather_around(): lax.ppermute(going_down, axis, [(d, (d - 1) % ways) for d in range(ways)])]
  transfers between devices with their start and end apart: 6 -> 12, of which waited for: 5 -> 9; matrix products, arithmetic and copies ran while one was open for 7% -> 8% of each run, Pallas kernels for 0% -> 0%
where the time goes in v1:
time: 232 us
  waiting for transfers between devices  157 us (68%)
  matrix products  35.8 us (15%)
  starting transfers between devices  22.8 us (10%)
  between operations  13.4 us (6%)
    reduce_scatter x1, waiting for transfers between devices, local(): lax.psum_scatter(product.reshape(col_count * lax.axis_size('tp'), row_cou...  75.6 us
    all_gather x1, waiting for transfers between devices, local(): lax.all_gather(down_weight, 'sp', axis=1, tiled=True)  36.8 us
    ppermute x4, waiting for transfers between devices, gather_around(): lax.ppermute(going_up, axis, [(d, (d + 1) % ways) for d in range(ways)])  20.2 us
    all_gather x1, waiting for transfers between devices, local(): lax.all_gather(up_weight, 'sp', axis=0, tiled=True)  19.2 us
    dot_general x1, matrix products, local(): jnp.dot(mixed.reshape(-1, hidden_dev), down_full, preferred_element_type=...  18 us
    dot_general x1, matrix products, local(): jnp.dot(flat_piece, up_full, preferred_element_type=jnp.float32) + up_bias  17.8 us
    ppermute x3, starting transfers between devices, gather_around(): lax.ppermute(going_down, axis, [(d, (d - 1) % ways) for d in range(ways)])  10.5 us
    ppermute x4, starting transfers between devices, gather_around(): lax.ppermute(going_up, axis, [(d, (d + 1) % ways) for d in range(ways)])  9.03 us
  transfers between devices with their start and end apart: 12, of which 9 were waited for; matrix products, arithmetic and copies ran while one was open for 8% of the time, Pallas kernels for 0%

profile of v1, /device:TPU:0, one launch (start us, length us, event | category | flops | bytes accessed | tf_op | source)
XLA Modules:
  0.0 231.8 jit_solution(2769930759722239279)
XLA Ops:
  6.5 0.0 all-gather.3.cloned.1.call-start
  6.5 0.7 all-gather.3.cloned.1.call-update
  7.3 0.0 copy-start
  7.3 0.0 all-gather.5.cloned.1.call-start
  7.3 0.7 all-gather.5.cloned.1.call-update
  8.0 0.0 reduce-scatter.2.cloned.1.call-start
  8.1 0.1 copy-done
  8.2 3.0 %collective-permute-start = (bf16[1,16,6144]{2,1,0:T(8,128)(2,1)S(1)}, bf16[1,16,6144]{2,1,0:T(8,128)(2,1)S(1)}, u32[]{:S(2)}, u32[]{:S(2)}) collective-permute-start(bf16[1,16,6144]{2,1,0:T(8,128)(2,1)S(1)} %copy-done), channel_id=1, source_target_pairs={{0,1},{1,2},{2,3},{3,4},{4,5},{5,6},{6,7},{7,0},{8,9},{9,10},{10,1... | collective-permute-start | bytes 589832 | tf_op jit(solution)/shard_map/ppermute | solution.py:15
  11.2 3.0 %collective-permute-start.1 = (bf16[1,16,6144]{2,1,0:T(8,128)(2,1)S(1)}, bf16[1,16,6144]{2,1,0:T(8,128)(2,1)S(1)}, u32[]{:S(2)}, u32[]{:S(2)}) collective-permute-start(bf16[1,16,6144]{2,1,0:T(8,128)(2,1)S(1)} %copy-done), channel_id=1, source_target_pairs={{0,7},{1,0},{2,1},{3,2},{4,3},{5,4},{6,5},{7,6},{8,15},{9,8},{10,9... | collective-permute-start | bytes 589832 | tf_op jit(solution)/shard_map/ppermute | solution.py:18
  14.2 0.1 broadcast_in_dim.2
  14.4 0.0 copy-start.3
  14.5 5.0 %collective-permute-done = bf16[1,16,6144]{2,1,0:T(8,128)(2,1)S(1)} collective-permute-done((bf16[1,16,6144]{2,1,0:T(8,128)(2,1)S(1)}, bf16[1,16,6144]{2,1,0:T(8,128)(2,1)S(1)}, u32[]{:S(2)}, u32[]{:S(2)}) %collective-permute-start) | collective-permute-done | bytes 196640 | tf_op jit(solution)/shard_map/ppermute | solution.py:15
  19.5 2.5 %collective-permute-start.2 = (bf16[1,16,6144]{2,1,0:T(8,128)(2,1)S(1)}, bf16[1,16,6144]{2,1,0:T(8,128)(2,1)S(1)}, u32[]{:S(2)}, u32[]{:S(2)}) collective-permute-start(bf16[1,16,6144]{2,1,0:T(8,128)(2,1)S(1)} %collective-permute-done), channel_id=1, source_target_pairs={{0,1},{1,2},{2,3},{3,4},{4,5},{5,6},{6,7},{7,0},{8,9},{9,10},{10,1... | collective-permute-start | bytes 589832 | tf_op jit(solution)/shard_map/ppermute | solution.py:15
  22.0 0.0 collective-permute-done.1
  22.0 3.0 %collective-permute-start.3 = (bf16[1,16,6144]{2,1,0:T(8,128)(2,1)S(1)}, bf16[1,16,6144]{2,1,0:T(8,128)(2,1)S(1)}, u32[]{:S(2)}, u32[]{:S(2)}) collective-permute-start(bf16[1,16,6144]{2,1,0:T(8,128)(2,1)S(1)} %collective-permute-done.1), channel_id=1, source_target_pairs={{0,7},{1,0},{2,1},{3,2},{4,3},{5,4},{6,5},{7,6},{8,15},{9,8},{10,9... | collective-permute-start | bytes 589832 | tf_op jit(solution)/shard_map/ppermute | solution.py:18
  25.1 4.4 %collective-permute-done.2 = bf16[1,16,6144]{2,1,0:T(8,128)(2,1)S(1)} collective-permute-done((bf16[1,16,6144]{2,1,0:T(8,128)(2,1)S(1)}, bf16[1,16,6144]{2,1,0:T(8,128)(2,1)S(1)}, u32[]{:S(2)}, u32[]{:S(2)}) %collective-permute-start.2) | collective-permute-done | bytes 196640 | tf_op jit(solution)/shard_map/ppermute | solution.py:15
  29.5 2.5 %collective-permute-start.4 = (bf16[1,16,6144]{2,1,0:T(8,128)(2,1)S(1)}, bf16[1,16,6144]{2,1,0:T(8,128)(2,1)S(1)}, u32[]{:S(2)}, u32[]{:S(2)}) collective-permute-start(bf16[1,16,6144]{2,1,0:T(8,128)(2,1)S(1)} %collective-permute-done.2), channel_id=1, source_target_pairs={{0,1},{1,2},{2,3},{3,4},{4,5},{5,6},{6,7},{7,0},{8,9},{9,10},{10,1... | collective-permute-start | bytes 589832 | tf_op jit(solution)/shard_map/ppermute | solution.py:15
  32.0 0.0 collective-permute-done.3
  32.0 4.4 %collective-permute-start.5 = (bf16[1,16,6144]{2,1,0:T(8,128)(2,1)S(1)}, bf16[1,16,6144]{2,1,0:T(8,128)(2,1)S(1)}, u32[]{:S(2)}, u32[]{:S(2)}) collective-permute-start(bf16[1,16,6144]{2,1,0:T(8,128)(2,1)S(1)} %collective-permute-done.3), channel_id=1, source_target_pairs={{0,7},{1,0},{2,1},{3,2},{4,3},{5,4},{6,5},{7,6},{8,15},{9,8},{10,9... | collective-permute-start | bytes 589832 | tf_op jit(solution)/shard_map/ppermute | solution.py:18
  36.4 3.7 %collective-permute-done.4 = bf16[1,16,6144]{2,1,0:T(8,128)(2,1)S(1)} collective-permute-done((bf16[1,16,6144]{2,1,0:T(8,128)(2,1)S(1)}, bf16[1,16,6144]{2,1,0:T(8,128)(2,1)S(1)}, u32[]{:S(2)}, u32[]{:S(2)}) %collective-permute-start.4) | collective-permute-done | bytes 196640 | tf_op jit(solution)/shard_map/ppermute | solution.py:15
  40.1 1.1 collective-permute-start.6
  41.2 2.0 collective-permute-done.5
  43.2 7.0 %collective-permute-done.6 = bf16[1,16,6144]{2,1,0:T(8,128)(2,1)S(1)} collective-permute-done((bf16[1,16,6144]{2,1,0:T(8,128)(2,1)S(1)}, bf16[1,16,6144]{2,1,0:T(8,128)(2,1)S(1)}, u32[]{:S(2)}, u32[]{:S(2)}) %collective-permute-start.6) | collective-permute-done | bytes 196640 | tf_op jit(solution)/shard_map/ppermute | solution.py:15
  50.3 19.2 %all-gather.3.cloned.1.call-done = bf16[6144,3072]{1,0:T(8,128)(2,1)} async-done(((bf16[3072,3072]{1,0:T(8,128)(2,1)}), bf16[6144,3072]{1,0:T(8,128)(2,1)}) %all-gather.3.cloned.1.call-update) | async-done | bytes 37748752 | tf_op jit(solution)/shard_map/all_gather | solution.py:57
  69.5 0.0 copy-done.3
  69.5 0.0 copy-start.1
  69.5 17.8 %fusion.2 = bf16[128,3072]{1,0:T(8,128)(2,1)S(1)} fusion(bf16[128,6144]{1,0:T(8,128)(2,1)S(1)} %bitcast.16, bf16[6144,3072]{1,0:T(8,128)(2,1)} %all-gather.3.cloned.1.call-done, f32[3072]{0:T(1024)S(1)} %copy-done.3), kind=kOutput, calls=%fused_computation.5 | convolution fusion | flops 4832624640 | bytes 40120320 | tf_op jit(solution)/shard_map/dot_general | solution.py:62
  87.3 0.0 copy-start.4
  87.3 0.2 fusion.99
  87.5 2.0 collective-permute-start.7
  89.4 1.3 collective-permute-start.8
  90.7 0.0 copy-done.1
  90.8 0.1 fusion.100
  90.8 0.0 collective-permute-done.7
  90.9 1.8 collective-permute-done.8
  92.6 0.5 fusion.18
  93.1 36.8 %all-gather.5.cloned.1.call-done = bf16[3072,6144]{1,0:T(8,128)(2,1)} async-done(((bf16[3072,3072]{1,0:T(8,128)(2,1)}), bf16[3072,6144]{1,0:T(8,128)(2,1)}) %all-gather.5.cloned.1.call-update) | async-done | bytes 37748752 | tf_op jit(solution)/shard_map/all_gather | solution.py:58
  130.0 0.0 copy-done.4
  130.0 18.0 %fusion = f32[8,16,6144]{2,1,0:T(8,128)} fusion(bf16[3072,6144]{1,0:T(8,128)(2,1)} %all-gather.5.cloned.1.call-done, bf16[8,16,3072]{2,1,0:T(8,128)(2,1)S(1)} %bitcast.19, bf16[10,18,3072]{2,1,0:T(8,128)(2,1)S(1)} %fusion.18, bf16[8,1,3072]{2,1,0:T(2,128)(2,1)S(1)} %collective-permute-done.8, bf16[8,1,3072]{2,1,0:T(2,128)(2,1)S(1)} %collective-permute-done.7, ...), kind=kOutput, calls=%fused_computation | convolution fusion | flops 4870373376 | bytes 46718976 | tf_op jit(solution)/shard_map/dot_general | solution.py:65
  147.9 0.0 copy-start.2
  147.9 0.0 reduce-scatter.2.cloned.1.call-update
  148.0 75.6 %reduce-scatter.2.cloned.1.call-done = f32[1,16,6144]{2,1,0:T(8,128)} async-done(((f32[8,16,6144]{2,1,0:T(8,128)}), f32[1,16,6144]{2,1,0:T(8,128)}) %reduce-scatter.2.cloned.1.call-update) | async-done | bytes 393232 | tf_op jit(solution)/shard_map/reduce_scatter | solution.py:66
  223.6 0.0 copy-done.2
  223.6 1.7 add_convert_fusion
  (8 shorter events, 0.1 us)
Async XLA Ops:
  6.5 62.9 %all-gather.3.cloned.1.call-start = ((), (), s32[]{:S(2)}) async-start(), calls=%async_computation.1 | async-start | bytes 56623104 | tf_op jit(solution)/shard_map/all_gather | solution.py:57
  7.3 0.9 copy-start
  7.3 122.7 %all-gather.5.cloned.1.call-start = ((), (), s32[]{:S(2)}) async-start(), calls=%async_computation.2 | async-start | bytes 56623104 | tf_op jit(solution)/shard_map/all_gather | solution.py:58
  8.0 215.5 %reduce-scatter.2.cloned.1.call-start = ((), (), s32[]{:S(2)}) async-start(), calls=%async_computation.3 | async-start | bytes 3538944 | tf_op jit(solution)/shard_map/reduce_scatter | solution.py:66
  8.2 11.3 %collective-permute-start = (bf16[1,16,6144]{2,1,0:T(8,128)(2,1)S(1)}, bf16[1,16,6144]{2,1,0:T(8,128)(2,1)S(1)}, u32[]{:S(2)}, u32[]{:S(2)}) collective-permute-start(bf16[1,16,6144]{2,1,0:T(8,128)(2,1)S(1)} %copy-done), channel_id=1, source_target_pairs={{0,1},{1,2},{2,3},{3,4},{4,5},{5,6},{6,7},{7,0},{8,9},{9,10},{10,1... | collective-permute-start | bytes 589832 | tf_op jit(solution)/shard_map/ppermute | solution.py:15
  11.2 10.9 %collective-permute-start.1 = (bf16[1,16,6144]{2,1,0:T(8,128)(2,1)S(1)}, bf16[1,16,6144]{2,1,0:T(8,128)(2,1)S(1)}, u32[]{:S(2)}, u32[]{:S(2)}) collective-permute-start(bf16[1,16,6144]{2,1,0:T(8,128)(2,1)S(1)} %copy-done), channel_id=1, source_target_pairs={{0,7},{1,0},{2,1},{3,2},{4,3},{5,4},{6,5},{7,6},{8,15},{9,8},{10,9... | collective-permute-start | bytes 589832 | tf_op jit(solution)/shard_map/ppermute | solution.py:18
  14.4 55.1 %copy-start.3 = (f32[3072]{0:T(1024)S(1)}, f32[3072]{0:T(1024)}, u32[]{:S(2)}) copy-start(f32[3072]{0:T(1024)} %param.9) | copy-start | bytes 36868
  19.5 10.0 %collective-permute-start.2 = (bf16[1,16,6144]{2,1,0:T(8,128)(2,1)S(1)}, bf16[1,16,6144]{2,1,0:T(8,128)(2,1)S(1)}, u32[]{:S(2)}, u32[]{:S(2)}) collective-permute-start(bf16[1,16,6144]{2,1,0:T(8,128)(2,1)S(1)} %collective-permute-done), channel_id=1, source_target_pairs={{0,1},{1,2},{2,3},{3,4},{4,5},{5,6},{6,7},{7,0},{8,9},{9,10},{10,1... | collective-permute-start | bytes 589832 | tf_op jit(solution)/shard_map/ppermute | solution.py:15
  22.0 10.0 %collective-permute-start.3 = (bf16[1,16,6144]{2,1,0:T(8,128)(2,1)S(1)}, bf16[1,16,6144]{2,1,0:T(8,128)(2,1)S(1)}, u32[]{:S(2)}, u32[]{:S(2)}) collective-permute-start(bf16[1,16,6144]{2,1,0:T(8,128)(2,1)S(1)} %collective-permute-done.1), channel_id=1, source_target_pairs={{0,7},{1,0},{2,1},{3,2},{4,3},{5,4},{6,5},{7,6},{8,15},{9,8},{10,9... | collective-permute-start | bytes 589832 | tf_op jit(solution)/shard_map/ppermute | solution.py:18
  29.5 10.6 %collective-permute-start.4 = (bf16[1,16,6144]{2,1,0:T(8,128)(2,1)S(1)}, bf16[1,16,6144]{2,1,0:T(8,128)(2,1)S(1)}, u32[]{:S(2)}, u32[]{:S(2)}) collective-permute-start(bf16[1,16,6144]{2,1,0:T(8,128)(2,1)S(1)} %collective-permute-done.2), channel_id=1, source_target_pairs={{0,1},{1,2},{2,3},{3,4},{4,5},{5,6},{6,7},{7,0},{8,9},{9,10},{10,1... | collective-permute-start | bytes 589832 | tf_op jit(solution)/shard_map/ppermute | solution.py:15
  32.0 11.2 %collective-permute-start.5 = (bf16[1,16,6144]{2,1,0:T(8,128)(2,1)S(1)}, bf16[1,16,6144]{2,1,0:T(8,128)(2,1)S(1)}, u32[]{:S(2)}, u32[]{:S(2)}) collective-permute-start(bf16[1,16,6144]{2,1,0:T(8,128)(2,1)S(1)} %collective-permute-done.3), channel_id=1, source_target_pairs={{0,7},{1,0},{2,1},{3,2},{4,3},{5,4},{6,5},{7,6},{8,15},{9,8},{10,9... | collective-permute-start | bytes 589832 | tf_op jit(solution)/shard_map/ppermute | solution.py:18
  40.1 10.1 %collective-permute-start.6 = (bf16[1,16,6144]{2,1,0:T(8,128)(2,1)S(1)}, bf16[1,16,6144]{2,1,0:T(8,128)(2,1)S(1)}, u32[]{:S(2)}, u32[]{:S(2)}) collective-permute-start(bf16[1,16,6144]{2,1,0:T(8,128)(2,1)S(1)} %collective-permute-done.4), channel_id=1, source_target_pairs={{0,1},{1,2},{2,3},{3,4},{4,5},{5,6},{6,7},{7,0},{8,9},{9,10},{10,1... | collective-permute-start | bytes 589832 | tf_op jit(solution)/shard_map/ppermute | solution.py:15
  69.5 21.3 %copy-start.1 = (f32[3,3,3072]{2,1,0:T(4,128)S(1)}, f32[3,3,3072]{2,1,0:T(4,128)}, u32[]{:S(2)}) copy-start(f32[3,3,3072]{2,1,0:T(4,128)} %param.10) | copy-start | bytes 331780
  87.3 42.7 %copy-start.4 = (f32[3072]{0:T(1024)S(1)}, f32[3072]{0:T(1024)}, u32[]{:S(2)}) copy-start(f32[3072]{0:T(1024)} %param.11) | copy-start | bytes 36868
  87.5 3.4 %collective-permute-start.7 = (bf16[8,1,3072]{2,1,0:T(2,128)(2,1)S(1)}, bf16[8,1,3072]{2,1,0:T(2,128)(2,1)S(1)}, u32[]{:S(2)}, u32[]{:S(2)}) collective-permute-start(bf16[8,1,3072]{2,1,0:T(2,128)(2,1)S(1)} %get-tuple-element.5), channel_id=1, source_target_pairs={{0,8},{1,9},{2,10},{3,11},{4,12},{5,13},{6,14},{7,15},{16,24},{17,... | collective-permute-start | bytes 147464 | tf_op jit(solution)/shard_map/ppermute | solution.py:30
  89.4 3.2 %collective-permute-start.8 = (bf16[8,1,3072]{2,1,0:T(2,128)(2,1)S(1)}, bf16[8,1,3072]{2,1,0:T(2,128)(2,1)S(1)}, u32[]{:S(2)}, u32[]{:S(2)}) collective-permute-start(bf16[8,1,3072]{2,1,0:T(2,128)(2,1)S(1)} %get-tuple-element.6), channel_id=1, source_target_pairs={{8,0},{9,1},{10,2},{11,3},{12,4},{13,5},{14,6},{15,7},{24,16},{25,... | collective-permute-start | bytes 147464 | tf_op jit(solution)/shard_map/ppermute | solution.py:33
  147.9 75.6 %copy-start.2 = (f32[6144]{0:T(1024)S(1)}, f32[6144]{0:T(1024)}, u32[]{:S(2)}) copy-start(f32[6144]{0:T(1024)} %param.13) | copy-start | bytes 73732
Sparse Core Ops, SparseCore 0:
  8.9 60.4 all-gather.2
  71.0 58.9 all-gather.4
  148.1 75.4 reduce-scatter.1
